TPU v7x, 256 devices: a whole 4x4x8 slice. The times are simulated.
256 devices in a mesh: section: 8 (over x, core), seq: 32 (over z, y).
Axes of the slice: x: 4, y: 4, z: 8, core: 2. Of those that a mesh axis runs over, the one named last changes fastest.
Arguments:
- queries: bfloat16 [8, 10240, 4096], P('section', 'seq'), may hold values from -60 to 60
- keys_new: bfloat16 [8, 10240, 4096], P('section', 'seq'), may hold values from -6 to 6
- values_new: bfloat16 [8, 10240, 4096], P('section', 'seq'), may hold values from -6 to 6
- keys_cache: bfloat16 [8, 6144, 4096], P('section', None, 'seq'), may hold values from -6 to 6
- values_cache: bfloat16 [8, 6144, 4096], P('section', None, 'seq'), may hold values from -6 to 6
- window: int32 [8, 32], P('section', 'seq'), may hold values from 1 to 3, as said below
- global_blocks: int32 [8, 2], P('section'), may hold values from 0 to 95
- random_blocks: int32 [8, 160, 3], P('section'), may hold values from 0 to 95
Outputs:
- handed: bfloat16 [8, 10240, 4096], P('section', 'seq')
Inputs may be any that keep to these rules, and one draw needn't show every extreme that they name: In every section some head has the window 3.
All inputs are finite; a program needn't handle non-finite values.
Results may differ from a plain program's by a relative error of at most 0.0049.
Values may be sent and summed in bfloat16 or wider, within the bound.
A program may use at most 128 MiB of HBM per device.

v0:
```python
import math

import jax
import jax.numpy as jnp
from jax import lax
from jax.sharding import PartitionSpec as P

HD = 128
BLK = 64
WMAX = 3
GLOB = 2
RAND = 3
NK = 8


masked_score = -1e30


def as_sent(shard):

    def short(part):
        return part.astype(jnp.bfloat16) if part.dtype == jnp.float32 else part

    return jax.tree.map(short, shard)


def passed_along(shard, axis, by):
    devices = lax.axis_size(axis)
    return lax.ppermute(shard, axis, [(i, (i + by) % devices) for i in range(devices)])


def block_mask(span_blocks):
    rows = jnp.arange(BLK, dtype=jnp.int32)[:, None]
    column = jnp.arange(NK * BLK, dtype=jnp.int32)[None, :]
    which = column // BLK
    inside = column % BLK
    allowed = jnp.where(which >= WMAX, True, which < span_blocks)
    return allowed & ((which != 0) | (inside <= rows))


def attend_local(
    query,
    fresh_keys,
    fresh_values,
    old_keys,
    old_values,
    span_blocks,
    global_row,
    random_rows,
    group,
):
    stretch_rows = query.shape[0]
    block_count = stretch_rows // BLK
    cache_blocks = old_keys.shape[0] // BLK
    lead = (WMAX - 1) * BLK
    near_keys = jnp.concatenate([old_keys[old_keys.shape[0] - lead :], fresh_keys], axis=0)
    near_values = jnp.concatenate([old_values[old_values.shape[0] - lead :], fresh_values], axis=0)
    glob_keys = jnp.concatenate(
        [lax.dynamic_slice_in_dim(old_keys, global_row[g] * BLK, BLK, 0) for g in range(GLOB)],
        axis=0,
    )
    glob_values = jnp.concatenate(
        [lax.dynamic_slice_in_dim(old_values, global_row[g] * BLK, BLK, 0) for g in range(GLOB)],
        axis=0,
    )
    key_blocks = old_keys.reshape(cache_blocks, BLK, HD)
    value_blocks = old_values.reshape(cache_blocks, BLK, HD)
    query_blocks = query.reshape(block_count, BLK, HD)
    allowed = block_mask(span_blocks)
    scale = 1.0 / math.sqrt(HD)

    def one_group(index):
        first = index * group
        query_part = lax.dynamic_slice_in_dim(query_blocks, first, group, 0)
        near_key_part = lax.dynamic_slice_in_dim(
            near_keys, first * BLK, (group + WMAX - 1) * BLK, 0
        )
        near_value_part = lax.dynamic_slice_in_dim(
            near_values, first * BLK, (group + WMAX - 1) * BLK, 0
        )
        random_part = lax.dynamic_slice_in_dim(random_rows, first, group, 0)
        rand_keys = key_blocks[random_part].reshape(group, RAND * BLK, HD)
        rand_values = value_blocks[random_part].reshape(group, RAND * BLK, HD)
        near_value_list = []
        pieces = []
        for slot in range(WMAX):
            offset = (WMAX - 1 - slot) * BLK
            slot_keys = near_key_part[offset : offset + group * BLK].reshape(group, BLK, HD)
            near_value_list.append(
                near_value_part[offset : offset + group * BLK].reshape(group, BLK, HD)
            )
            pieces.append(
                jnp.einsum(
                    "gih,gjh->gij", query_part, slot_keys, preferred_element_type=jnp.float32
                )
            )
        pieces.append(
            jnp.einsum("gih,jh->gij", query_part, glob_keys, preferred_element_type=jnp.float32)
        )
        pieces.append(
            jnp.einsum("gih,gjh->gij", query_part, rand_keys, preferred_element_type=jnp.float32)
        )
        scores = jnp.concatenate(pieces, axis=2) * scale
        scores = jnp.where(allowed[None], scores, masked_score)
        top = jnp.max(scores, axis=-1, keepdims=True)
        expo = jnp.exp(scores - top)
        weights = (expo / jnp.sum(expo, axis=-1, keepdims=True)).astype(jnp.bfloat16)
        result = jnp.einsum(
            "gij,gjh->gih",
            weights[:, :, WMAX * BLK + GLOB * BLK :],
            rand_values,
            preferred_element_type=jnp.float32,
        )
        result = result + jnp.einsum(
            "gij,jh->gih",
            weights[:, :, WMAX * BLK : WMAX * BLK + GLOB * BLK],
            glob_values,
            preferred_element_type=jnp.float32,
        )
        for slot in range(WMAX):
            result = result + jnp.einsum(
                "gij,gjh->gih",
                weights[:, :, slot * BLK : (slot + 1) * BLK],
                near_value_list[slot],
                preferred_element_type=jnp.float32,
            )
        return result.astype(jnp.bfloat16)

    outputs = lax.map(one_group, jnp.arange(block_count // group, dtype=jnp.int32))
    return outputs.reshape(stretch_rows, HD)


def per_device(
    queries, keys_new, values_new, keys_cache, values_cache, window, global_blocks, random_blocks
):
    head_queries = lax.all_to_all(queries, "seq", split_axis=2, concat_axis=1, tiled=True)
    head_keys, head_values = (
        lax.all_to_all(keys_new, "seq", split_axis=2, concat_axis=1, tiled=True),
        lax.all_to_all(values_new, "seq", split_axis=2, concat_axis=1, tiled=True),
    )
    stretch_rows = head_queries.shape[1]
    block_count = stretch_rows // BLK
    group = math.gcd(block_count, 8)
    global_row = global_blocks[0]
    random_rows = random_blocks[0]
    results = [
        attend_local(
            head_queries[0],
            head_keys[0],
            head_values[0],
            keys_cache[0],
            values_cache[0],
            window[0, 0],
            global_row,
            random_rows,
            group,
        )
    ]
    attended = jnp.concatenate(results, axis=1)[None]
    regrouped = lax.all_to_all(
        as_sent(attended), "seq", split_axis=1, concat_axis=2, tiled=True
    ).astype(attended.dtype)
    return passed_along(as_sent(regrouped), "section", 1).astype(regrouped.dtype)


def solution(mesh):
    placed = (
        P("section", "seq", None),
        P("section", "seq", None),
        P("section", "seq", None),
        P("section", None, "seq"),
        P("section", None, "seq"),
        P("section", "seq"),
        P("section", None),
        P("section", None, None),
    )
    return jax.shard_map(
        per_device, mesh=mesh, in_specs=placed, out_specs=P("section", "seq", None), check_vma=False
    )
```

profile of v0, /device:TPU:88, one launch (start us, length us, event | category | flops | bytes accessed | tf_op | source)
XLA Modules:
  0.0 885.9 jit_solution(13821503862325278436)
XLA Ops:
  0.0 14.3 %copy.46 = bf16[1,320,4096]{1,0,2:T(2,128)(2,1)} copy(bf16[1,320,4096]{2,1,0:T(8,128)(2,1)} %param.12) | data formatting | bytes 5242880 | tf_op args[2]
  14.9 67.0 %reduce.2 = bf16[4096,320]{1,0:T(8,128)(2,1)S(1)} reduce(bf16[4096,1,320]{2,1,0:T(2,128)(2,1)} %bitcast.118, bf16[]{:T(256)} %broadcast.139), dimensions={1}, to_apply=%bitcast.58.reduce_sub_computation | reduce | bytes 5242882
  81.9 4.4 reshape.177
  86.3 11.3 %all-to-all-start.2 = ((bf16[32,2,20480]{2,1,0:T(2,128)(2,1)}), bf16[32,2,20480]{2,1,0:T(2,128)(2,1)}, u32[]{:S(2)}, u32[]{:S(2)}) async-start(bf16[32,2,20480]{2,1,0:T(2,128)(2,1)} %reshape.177), calls=%async_computation.2 | async-start | bytes 5242880 | tf_op jit(solution)/shard_map/all_to_all | solution.py:139
  97.7 12.3 %copy.42 = bf16[1,320,4096]{1,0,2:T(2,128)(2,1)} copy(bf16[1,320,4096]{2,1,0:T(8,128)(2,1)S(1)} %copy-done.2) | data formatting | bytes 5242880 | tf_op args[1]
  110.0 67.0 %reduce.1 = bf16[4096,320]{1,0:T(8,128)(2,1)S(1)} reduce(bf16[4096,1,320]{2,1,0:T(2,128)(2,1)} %bitcast.122, bf16[]{:T(256)} %broadcast.139), dimensions={1}, to_apply=%bitcast.56.reduce_sub_computation | reduce | bytes 5242882
  177.1 4.3 reshape.175
  181.4 10.8 %all-to-all-start.1 = ((bf16[32,2,20480]{2,1,0:T(2,128)(2,1)}), bf16[32,2,20480]{2,1,0:T(2,128)(2,1)}, u32[]{:S(2)}, u32[]{:S(2)}) async-start(bf16[32,2,20480]{2,1,0:T(2,128)(2,1)} %reshape.175), calls=%async_computation.1 | async-start | bytes 5242880 | tf_op jit(solution)/shard_map/all_to_all | solution.py:138
  192.2 12.3 %copy.39 = bf16[1,320,4096]{1,0,2:T(2,128)(2,1)} copy(bf16[1,320,4096]{2,1,0:T(8,128)(2,1)S(1)} %copy-done.3) | data formatting | bytes 5242880 | tf_op args[0]
  204.6 67.0 %reduce = bf16[4096,320]{1,0:T(8,128)(2,1)S(1)} reduce(bf16[4096,1,320]{2,1,0:T(2,128)(2,1)} %bitcast.123, bf16[]{:T(256)} %broadcast.139), dimensions={1}, to_apply=%bitcast.54.reduce_sub_computation | reduce | bytes 5242882
  271.6 4.4 reshape.173
  276.0 10.3 %all-to-all-start = ((bf16[32,2,20480]{2,1,0:T(2,128)(2,1)}), bf16[32,2,20480]{2,1,0:T(2,128)(2,1)}, u32[]{:S(2)}, u32[]{:S(2)}) async-start(bf16[32,2,20480]{2,1,0:T(2,128)(2,1)} %reshape.173), calls=%async_computation | async-start | bytes 5242880 | tf_op jit(solution)/shard_map/all_to_all | solution.py:136
  291.3 19.9 %reshape.178 = bf16[4096,1,320]{2,1,0:T(2,128)(2,1)} reshape(bf16[32,2,20480]{2,1,0:T(2,128)(2,1)} %all-to-all-done.2) | data formatting | bytes 5242880
  311.2 3.3 copy.56
  314.5 3.2 copy.53
  317.8 4.2 copy.48
  322.0 19.9 %reshape.176 = bf16[4096,1,320]{2,1,0:T(2,128)(2,1)} reshape(bf16[32,2,20480]{2,1,0:T(2,128)(2,1)} %all-to-all-done.1) | data formatting | bytes 5242880
  341.9 3.3 copy.55
  345.2 3.2 copy.52
  348.4 4.3 copy.44
  352.8 19.9 %reshape.174 = bf16[4096,1,320]{2,1,0:T(2,128)(2,1)} reshape(bf16[32,2,20480]{2,1,0:T(2,128)(2,1)} %all-to-all-done) | data formatting | bytes 5242880
  372.7 3.3 copy.54
  376.0 3.3 copy.51
  379.3 4.4 copy.41
  383.7 2.6 pad_maximum_fusion
  386.3 322.0 %while.13 = (s32[]{:T(128)}, bf16[20,8,64,128]{3,2,1,0:T(8,128)(2,1)}, s32[20]{0:T(128)S(1)}, bf16[160,64,128]{2,1,0:T(8,128)(2,1)}, bf16[10368,128]{1,0:T(8,128...) while((s32[]{:T(128)}, ...), condition=%wide.region_3.4_spmd.clone, body=%wide.region_0.3_spmd.clone.sunk | while | flops 136218192 | bytes 15348233 | solution.py:129
  392.9 2.0 gather_fusion.1
  398.6 2.0 gather_fusion
  409.0 2.0 gather_fusion.1
  414.7 2.0 gather_fusion
  425.1 2.0 gather_fusion.1
  446.9 2.0 gather_fusion
  457.3 2.0 gather_fusion.1
  495.2 2.0 gather_fusion
  505.6 2.0 gather_fusion.1
  527.3 2.0 gather_fusion
  537.8 2.0 gather_fusion.1
  543.4 2.0 gather_fusion
  553.9 2.0 gather_fusion.1
  559.5 2.0 gather_fusion
  570.0 2.0 gather_fusion.1
  708.3 6.0 copy.62
  714.3 56.2 %reduce.3 = bf16[10240,128]{1,0:T(8,128)(2,1)S(1)} reduce(bf16[10240,1,128]{2,1,0:T(2,128)(2,1)} %bitcast.124, bf16[]{:T(256)} %broadcast.139), dimensions={1}, to_apply=%bitcast.72.reduce_sub_computation | reduce | bytes 5242882
  770.5 2.2 reshape.179
  772.7 68.0 %all_to_all.63 = bf16[32,2,20480]{2,1,0:T(2,128)(2,1)S(1)} all-to-all(bf16[32,2,20480]{2,1,0:T(2,128)(2,1)} %reshape.179), channel_id=1, replica_groups=mesh['section'=8,'seq'=32] {'seq'}, dimensions={0} | all-to-all | bytes 5242880 | tf_op jit(solution)/shard_map/all_to_all | solution.py:160
  840.8 7.2 reshape.180
  848.0 3.2 copy.57
  852.0 32.3 %collective-permute-done = bf16[1,320,4096]{2,1,0:T(8,128)(2,1)S(1)} collective-permute-done((bf16[1,320,4096]{2,1,0:T(8,128)(2,1)S(1)}, bf16[1,320,4096]{2,1,0:T(8,128)(2,1)S(1)}, u32[]{:S(2)}, u32[]{:S(2)}) %collective-permute-start) | collective-permute-done | bytes 2621472 | tf_op jit(solution)/shard_map/ppermute | solution.py:29
  (435 shorter events, 269.7 us)
Async XLA Ops:
  86.3 11.4 %copy-start.2 = (bf16[1,320,4096]{2,1,0:T(8,128)(2,1)S(1)}, bf16[1,320,4096]{2,1,0:T(8,128)(2,1)}, u32[]{:S(2)}) copy-start(bf16[1,320,4096]{2,1,0:T(8,128)(2,1)} %param.11) | copy-start | bytes 7864324
  86.3 95.1 %all-to-all-start.2 = ((bf16[32,2,20480]{2,1,0:T(2,128)(2,1)}), bf16[32,2,20480]{2,1,0:T(2,128)(2,1)}, u32[]{:S(2)}, u32[]{:S(2)}) async-start(bf16[32,2,20480]{2,1,0:T(2,128)(2,1)} %reshape.177), calls=%async_computation.2 | async-start | bytes 5242880 | tf_op jit(solution)/shard_map/all_to_all | solution.py:139
  181.4 10.8 %copy-start.3 = (bf16[1,320,4096]{2,1,0:T(8,128)(2,1)S(1)}, bf16[1,320,4096]{2,1,0:T(8,128)(2,1)}, u32[]{:S(2)}) copy-start(bf16[1,320,4096]{2,1,0:T(8,128)(2,1)} %param.10) | copy-start | bytes 7864324
  181.4 94.6 %all-to-all-start.1 = ((bf16[32,2,20480]{2,1,0:T(2,128)(2,1)}), bf16[32,2,20480]{2,1,0:T(2,128)(2,1)}, u32[]{:S(2)}, u32[]{:S(2)}) async-start(bf16[32,2,20480]{2,1,0:T(2,128)(2,1)} %reshape.175), calls=%async_computation.1 | async-start | bytes 5242880 | tf_op jit(solution)/shard_map/all_to_all | solution.py:138
  276.0 10.3 %copy-start.5 = (s32[1,2]{1,0:T(1,128)S(1)}, s32[1,2]{1,0:T(1,128)}, u32[]{:S(2)}) copy-start(s32[1,2]{1,0:T(1,128)} %param.16) | copy-start | bytes 28
  276.0 12.9 %copy-start.4 = (s32[1,160,3]{1,0,2:T(1,128)S(1)}, s32[1,160,3]{1,0,2:T(1,128)}, u32[]{:S(2)}) copy-start(s32[1,160,3]{1,0,2:T(1,128)} %param.17) | copy-start | bytes 5764
  276.0 76.8 %all-to-all-start = ((bf16[32,2,20480]{2,1,0:T(2,128)(2,1)}), bf16[32,2,20480]{2,1,0:T(2,128)(2,1)}, u32[]{:S(2)}, u32[]{:S(2)}) async-start(bf16[32,2,20480]{2,1,0:T(2,128)(2,1)} %reshape.173), calls=%async_computation | async-start | bytes 5242880 | tf_op jit(solution)/shard_map/all_to_all | solution.py:136
  379.3 4.4 copy-start
  379.3 4.4 copy-start.1
  851.9 32.3 %collective-permute-start = (bf16[1,320,4096]{2,1,0:T(8,128)(2,1)S(1)}, bf16[1,320,4096]{2,1,0:T(8,128)(2,1)S(1)}, u32[]{:S(2)}, u32[]{:S(2)}) collective-permute-start(bf16[1,320,4096]{2,1,0:T(8,128)(2,1)S(1)} %bitcast.143), channel_id=1, source_target_pairs={{0,32},{32,64},{64,96},{96,128},{128,160},{160,192},{192,224},{224... | collective-permute-start | bytes 7864328 | tf_op jit(solution)/shard_map/ppermute | solution.py:29
where the time goes:
time: 903 us; the launch traced here: 886 us
  local copies, waits for them, and re-layouts  304 us (34%)
  other arithmetic  271 us (30%)
  matrix products  148 us (16%)
  blocking collectives  68 us (8%)
  starting transfers between devices  32.5 us (4%)
  waiting for transfers between devices  32.3 us (4%)
  loops' own time  27.7 us (3%)
    unnamed x4, other arithmetic  257 us
    unnamed x30, local copies, waits for them, and re-layouts  137 us
    all_to_all x1, blocking collectives, per_device(): lax.all_to_all(as_sent(attended), 'seq', split_axis=1, concat_axis=2, til...  68 us
    dot_general x60, matrix products, one_group(): jnp.einsum('gih,gjh->gij', query_part, slot_keys, preferred_element_type=...  65.6 us
    gather x20, local copies, waits for them, and re-layouts, one_group(): rand_keys = key_blocks[random_part].reshape(group, RAND * BLK, HD)  40.6 us
    gather x20, local copies, waits for them, and re-layouts, one_group(): rand_values = value_blocks[random_part].reshape(group, RAND * BLK, HD)  40.6 us
    ppermute x1, waiting for transfers between devices, passed_along(): lax.ppermute(shard, axis, [(i, (i + by) % devices) for i in range(devices)])  32.3 us
    another operation x1, loops' own time, attend_local(): lax.map(one_group, jnp.arange(block_count // group, dtype=jnp.int32))  27.7 us
  transfers between devices with their start and end apart: 4, of which 1 were waited for; matrix products, arithmetic and copies ran while one was open for 26% of the time, Pallas kernels for 0%

commit v1 on v0

v1 whole, which is shorter than its diff:
```python
import functools
import math

import jax
import jax.numpy as jnp
from jax import lax
from jax.experimental import pallas as pl
from jax.experimental.pallas import tpu as pltpu
from jax.sharding import PartitionSpec as P

HD = 128
BLK = 64
WMAX = 3
GLOB = 2
RAND = 3
LEAD = (WMAX - 1) * BLK
STAT = 16

MESH = pl.DeviceIdType.MESH
SCALE2 = math.log2(math.e) / math.sqrt(HD)
MASKED = -1e30


def signed_step(j, size):
    half = lax.div(j + 1, 2)
    odd = lax.rem(j, 2)
    return lax.rem(half * (2 * odd - 1) + size, size)


def nt_dot(a, b):
    return lax.dot_general(a, b, (((1,), (1,)), ((), ())), preferred_element_type=jnp.float32)


def kernel(
    n,
    ny,
    sections,
    q_hbm,
    k_hbm,
    v_hbm,
    kc_hbm,
    vc_hbm,
    win_ref,
    glob_ref,
    rand_ref,
    out_hbm,
    qv,
    kall,
    vall,
    kcv,
    vcv,
    qbuf,
    obuf,
    ogbuf,
    owbuf,
    lwbuf,
    fbuf,
    wbuf,
    thr,
    loc_sem,
    qrecv,
    orecv,
    qsend,
    osend,
    fsend,
    frecv,
    wsend,
    wrecv,
    hrecv,
    hsend,
    tsend,
):
    nz = n // ny
    rows = q_hbm.shape[1]
    cached = kc_hbm.shape[1]
    nb = rows // BLK
    sec = lax.axis_index("section")
    me = lax.axis_index("seq")
    z, y = lax.div(me, ny), lax.rem(me, ny)

    def at(i, back):
        dz = signed_step(lax.rem(i, nz), nz)
        dy = signed_step(lax.div(i, nz), ny)
        if back:
            dz, dy = nz - dz, ny - dy
        return lax.rem(z + dz, nz) * ny + lax.rem(y + dy, ny)

    def peer(i):
        return at(i, False)

    def source(i):
        return at(i, True)

    def columns(h):
        return pl.ds(pl.multiple_of(h * HD, HD), HD)

    def remote(src, dst, send, recv, seq, section=None):
        where = {"section": sec if section is None else section, "seq": seq}
        return pltpu.make_async_remote_copy(
            src_ref=src, dst_ref=dst, send_sem=send, recv_sem=recv, device_id=where, device_id_type=MESH
        )

    after = lax.rem(sec + 1, sections)
    before = lax.rem(sec + sections - 1, sections)

    local = [
        pltpu.make_async_copy(q_hbm.at[0], qv, loc_sem.at[0]),
        pltpu.make_async_copy(k_hbm.at[0], kall.at[pl.ds(LEAD, rows)], loc_sem.at[1]),
        pltpu.make_async_copy(v_hbm.at[0], vall.at[pl.ds(LEAD, rows)], loc_sem.at[2]),
        pltpu.make_async_copy(kc_hbm.at[0], kcv, loc_sem.at[3]),
        pltpu.make_async_copy(vc_hbm.at[0], vcv, loc_sem.at[4]),
    ]
    for copy in local:
        copy.start()
    pltpu.make_async_copy(q_hbm.at[0, :, columns(me)], qbuf.at[0], qrecv.at[0]).start()

    wbuf[0] = jnp.full((8, HD), win_ref[0, 0].astype(jnp.float32))

    barrier = pltpu.get_barrier_semaphore()

    def greet(i, carry):
        pl.semaphore_signal(barrier, 1, device_id={"section": sec, "seq": peer(i)}, device_id_type=MESH)
        return carry

    lax.fori_loop(1, n, greet, 0)
    for other in (after, before):
        pl.semaphore_signal(barrier, 1, device_id={"section": other, "seq": me}, device_id_type=MESH)
    pl.semaphore_wait(barrier, n + 1)

    def send_queries(i, carry):
        p = peer(i)
        remote(wbuf.at[0], wbuf.at[i], wsend, wrecv, p).start()
        remote(q_hbm.at[0, :, columns(p)], qbuf.at[i], qsend, qrecv.at[i], p).start()
        return carry

    lax.fori_loop(1, n, send_queries, 0)

    halo = []
    tail = []
    own_tail = []
    for j, (fresh, cache, whole) in enumerate(((k_hbm, kc_hbm, kall), (v_hbm, vc_hbm, vall))):
        halo.append(
            remote(
                fresh.at[0, pl.ds(rows - LEAD, LEAD)],
                whole.at[pl.ds(0, LEAD)],
                hsend.at[j],
                hrecv.at[j],
                lax.rem(me + 1, n),
            )
        )
        for w in range(WMAX - 1):
            block = cache.at[0, cached - WMAX + 1 + w]
            place = pl.ds(w * BLK, BLK)
            tail.append(
                remote(block, whole.at[place, columns(me)], tsend.at[j, w], hrecv.at[j], 0)
            )
            own_tail.append(
                pltpu.make_async_copy(block, whole.at[place, pl.ds(0, HD)], hrecv.at[j])
            )

    @pl.when(me < n - 1)
    def _():
        for copy in halo:
            copy.start()

    @pl.when(me > 0)
    def _():
        for copy in tail:
            copy.start()

    @pl.when(me == 0)
    def _():
        for copy in own_tail:
            copy.start()

    row = lax.broadcasted_iota(jnp.int32, (BLK, WMAX * BLK), 0)
    col = lax.broadcasted_iota(jnp.int32, (BLK, WMAX * BLK), 1)
    late = col - (WMAX - 1) * BLK > row
    width = jnp.where(col < BLK, 3.0, jnp.where(col < 2 * BLK, 2.0, jnp.where(late, 99.0, 1.0)))
    thr[...] = width

    def window_part(i, blocks):
        h = source(i)
        span = wbuf[i, 0:1, 0:1]
        allowed = thr[...] <= span
        for b in blocks:
            q = qv[b * BLK : (b + 1) * BLK, columns(h)]
            k = kall[b * BLK : b * BLK + WMAX * BLK, columns(h)]
            v = vall[b * BLK : b * BLK + WMAX * BLK, columns(h)]
            s = jnp.where(allowed, nt_dot(q, k), MASKED)
            top = jnp.max(s, axis=1, keepdims=True)
            e = jnp.exp2((s - top) * SCALE2)
            total = jnp.sum(e, axis=1, keepdims=True)
            o = jnp.dot(e.astype(jnp.bfloat16), v, preferred_element_type=jnp.float32)
            owbuf[h, b * BLK : (b + 1) * BLK, :] = o / total
            lwbuf[h, b * BLK : (b + 1) * BLK, :] = jnp.broadcast_to(
                top * SCALE2 + jnp.log2(total), (BLK, HD)
            )

    def inner_window(i, carry):
        window_part(i, range(WMAX - 1, nb))
        return carry

    def edge_window(i, carry):
        window_part(i, range(WMAX - 1))
        return carry

    for copy in local[:3]:
        copy.wait()
    pltpu.make_async_copy(wbuf.at[pl.ds(1, n - 1)], wbuf.at[pl.ds(1, n - 1)], wrecv).wait()
    lax.fori_loop(0, n, inner_window, 0)

    for copy in local[3:]:
        copy.wait()

    diagonal = lax.broadcasted_iota(jnp.int32, (BLK, HD), 0) == lax.broadcasted_iota(
        jnp.int32, (BLK, HD), 1
    )
    stat_row = lax.broadcasted_iota(jnp.int32, (STAT, HD), 0)

    def far_part(i, carry):
        src = source(i)
        pltpu.make_async_copy(qbuf.at[i], qbuf.at[i], qrecv.at[i]).wait()
        stats = jnp.zeros((STAT, HD), jnp.float32)
        for b in range(nb):
            picks = [glob_ref[0, g] for g in range(GLOB)] + [
                rand_ref[0, src * nb + b, r] for r in range(RAND)
            ]
            k = jnp.concatenate([kcv[x] for x in picks], axis=0)
            v = jnp.concatenate([vcv[x] for x in picks], axis=0)
            s = nt_dot(qbuf[i, b * BLK : (b + 1) * BLK, :], k)
            top = jnp.max(s, axis=1, keepdims=True)
            e = jnp.exp2((s - top) * SCALE2)
            total = jnp.sum(e, axis=1, keepdims=True)
            o = jnp.dot(e.astype(jnp.bfloat16), v, preferred_element_type=jnp.float32)
            obuf[i, b * BLK : (b + 1) * BLK, :] = (o / total).astype(jnp.bfloat16)
            lse = top * SCALE2 + jnp.log2(total)
            line = jnp.sum(jnp.where(diagonal, lse, 0.0), axis=0, keepdims=True)
            for part in range(3):
                piece = line.astype(jnp.bfloat16).astype(jnp.float32)
                stats = jnp.where(stat_row == part * nb + b, piece, stats)
                line = line - piece
        obuf[i, nb * BLK : nb * BLK + STAT, :] = stats.astype(jnp.bfloat16)

        @pl.when(i > 0)
        def _():
            remote(obuf.at[i], ogbuf.at[i], osend, orecv.at[i], src).start()

        @pl.when(i == 0)
        def _():
            pltpu.make_async_copy(obuf.at[i], ogbuf.at[i], orecv.at[i]).start()

        return carry

    lax.fori_loop(0, n, far_part, 0)

    for j, whole in enumerate((kall, vall)):
        pltpu.make_async_copy(whole.at[pl.ds(0, LEAD)], whole.at[pl.ds(0, LEAD)], hrecv.at[j]).wait()
    lax.fori_loop(0, n, edge_window, 0)

    def join(i, carry):
        h = peer(i)
        pltpu.make_async_copy(ogbuf.at[i], ogbuf.at[i], orecv.at[i]).wait()
        stats = ogbuf[i, nb * BLK : nb * BLK + STAT, :].astype(jnp.float32)
        for b in range(nb):
            line = (stats[b : b + 1] + stats[nb + b : nb + b + 1]) + stats[2 * nb + b : 2 * nb + b + 1]
            far = jnp.sum(jnp.where(diagonal, line, 0.0), axis=1, keepdims=True)
            near = lwbuf[h, b * BLK : (b + 1) * BLK, :]
            share = 1.0 / (1.0 + jnp.exp2(near - far))
            ow = owbuf[h, b * BLK : (b + 1) * BLK, :]
            og = ogbuf[i, b * BLK : (b + 1) * BLK, :].astype(jnp.float32)
            fbuf[i, b * BLK : (b + 1) * BLK, :] = (ow + share * (og - ow)).astype(jnp.bfloat16)
        remote(fbuf.at[i], out_hbm.at[0, :, columns(h)], fsend, frecv, me, after).start()
        return carry

    lax.fori_loop(0, n, join, 0)

    pltpu.make_async_copy(wbuf.at[pl.ds(1, n - 1)], wbuf.at[pl.ds(1, n - 1)], wsend).wait()
    pltpu.make_async_copy(qbuf.at[pl.ds(1, n - 1)], qbuf.at[pl.ds(1, n - 1)], qsend).wait()
    pltpu.make_async_copy(obuf.at[pl.ds(1, n - 1)], obuf.at[pl.ds(1, n - 1)], osend).wait()
    pltpu.make_async_copy(fbuf, fbuf, fsend).wait()
    pltpu.make_async_copy(out_hbm.at[0], out_hbm.at[0], frecv).wait()

    @pl.when(me < n - 1)
    def _():
        for copy in halo:
            copy.wait_send()

    @pl.when(me > 0)
    def _():
        for copy in tail:
            copy.wait_send()


def per_device(n, ny, sections, q, k, v, kc, vc, window, glob, rand):
    rows, wide = q.shape[1:]
    cached = kc.shape[1] // BLK
    kc, vc = (cache.reshape(1, cached, BLK, HD) for cache in (kc, vc))
    any_space = pl.BlockSpec(memory_space=pl.ANY)
    smem = pl.BlockSpec(memory_space=pltpu.SMEM)
    bf, f32, dma = jnp.bfloat16, jnp.float32, pltpu.SemaphoreType.DMA
    return pl.pallas_call(
        functools.partial(kernel, n, ny, sections),
        out_shape=jax.ShapeDtypeStruct(q.shape, bf),
        in_specs=[any_space] * 5 + [smem] * 3,
        out_specs=any_space,
        scratch_shapes=[
            pltpu.VMEM((rows, wide), bf),
            pltpu.VMEM((rows + LEAD, wide), bf),
            pltpu.VMEM((rows + LEAD, wide), bf),
            pltpu.VMEM((cached, BLK, HD), bf),
            pltpu.VMEM((cached, BLK, HD), bf),
            pltpu.VMEM((n, rows, HD), bf),
            pltpu.VMEM((n, rows + STAT, HD), bf),
            pltpu.VMEM((n, rows + STAT, HD), bf),
            pltpu.VMEM((n, rows, HD), f32),
            pltpu.VMEM((n, rows, HD), f32),
            pltpu.VMEM((n, rows, HD), bf),
            pltpu.VMEM((n, 8, HD), f32),
            pltpu.VMEM((BLK, WMAX * BLK), f32),
            dma((5,)),
            dma((n,)),
            dma((n,)),
            dma,
            dma,
            dma,
            dma,
            dma,
            dma,
            dma((2,)),
            dma((2,)),
            dma((2, WMAX - 1)),
        ],
        compiler_params=pltpu.CompilerParams(
            collective_id=0, has_side_effects=True, vmem_limit_bytes=56 * 1024 * 1024
        ),
    )(q, k, v, kc, vc, window, glob, rand)


def solution(mesh):
    n, sections = mesh.shape["seq"], mesh.shape["section"]
    ny = math.gcd(n, 4)
    placed = (
        P("section", "seq", None),
        P("section", "seq", None),
        P("section", "seq", None),
        P("section", None, "seq"),
        P("section", None, "seq"),
        P("section", "seq"),
        P("section", None),
        P("section", None, None),
    )
    return jax.shard_map(
        functools.partial(per_device, n, ny, sections),
        mesh=mesh,
        in_specs=placed,
        out_specs=P("section", "seq", None),
        check_vma=False,
    )
```

time: 903 us -> 200 us (0.22); the launches traced: 886 us -> 198 us
  local copies, waits for them, and re-layouts: 304 us -> 4.96 us
  other arithmetic: 271 us -> 0 us
  Pallas kernels: 0 us -> 192 us
  matrix products: 148 us -> 0 us
  blocking collectives: 68 us -> 0 us
  starting transfers between devices: 32.5 us -> 0 us
  waiting for transfers between devices: 32.3 us -> 0 us
  loops' own time: 27.7 us -> 0 us
    unnamed x4 -> x0, other arithmetic: 257 us -> none
    pallas_call x0 -> x1, Pallas kernels: none -> 192 us  [per_device(): pl.pallas_call(functools.partial(kernel, n, ny, sections), out_shape=jax....]
    dot_general x200 -> x0, matrix products: 148 us -> none  [the longest x60 65.6 us: one_group(): jnp.einsum('gih,gjh->gij', query_part, slot_keys, preferred_element_type=...]
    unnamed x30 -> x2, local copies, waits for them, and re-layouts: 137 us -> 4.96 us
    gather x40 -> x0, local copies, waits for them, and re-layouts: 81.2 us -> none  [the longest x20 40.6 us: one_group(): rand_keys = key_blocks[random_part].reshape(group, RAND * BLK, HD)]
    all_to_all x1 -> x0, blocking collectives: 68 us -> none  [per_device(): lax.all_to_all(as_sent(attended), 'seq', split_axis=1, concat_axis=2, til...]
    all_to_all x3 -> x0, starting transfers between devices: 32.5 us -> none  [the longest x1 11.3 us: per_device(): lax.all_to_all(values_new, 'seq', split_axis=2, concat_axis=1, tiled=True)]
    ppermute x1 -> x0, waiting for transfers between devices: 32.3 us -> none  [passed_along(): lax.ppermute(shard, axis, [(i, (i + by) % devices) for i in range(devices)])]
  transfers between devices with their start and end apart: 4 -> 0, of which waited for: 1 -> 0; matrix products, arithmetic and copies ran while one was open for 26% -> 0% of each run, Pallas kernels for 0% -> 0%
where the time goes in v1:
time: 200 us; the launch traced here: 198 us
  Pallas kernels  192 us (96%)
  local copies, waits for them, and re-layouts  4.96 us (2%)
    pallas_call x1, Pallas kernels, per_device(): pl.pallas_call(functools.partial(kernel, n, ny, sections), out_shape=jax....  192 us
    unnamed x2, local copies, waits for them, and re-layouts  4.96 us

profile of v1, /device:TPU:88, one launch (start us, length us, event | category | flops | bytes accessed | tf_op | source)
XLA Modules:
  0.0 197.9 jit_solution(9725601373953645599)
XLA Ops:
  0.7 1.4 copy.9.rand_ref
  2.1 192.2 %shard_map.82 = bf16[1,320,4096]{2,1,0:T(8,128)(2,1)} custom-call(bf16[1,320,4096]{2,1,0:T(8,128)(2,1)} %q_hbm.1, bf16[1,320,4096]{2,1,0:T(8,128)(2,1)} %k_hbm.1, bf16[1,320,4096]{2,1,0:T(8,128)(2,1)} %v_hbm.1, bf16[1,96,64,128]{3,2,1,0:T(8,128)(2,1)} %bitcast.2, bf16[1,96,64,128]{3,2,1,0:T(8,128)(2,1)} %bitcast.3, s32[1,1]{1,0:T(1,128)S(6)} %copy.11.win_ref, ...), custom_call_target="tpu_custom_call" | custom-call | tf_op jit(solution)/shard_map/pallas_call | solution.py:302
  194.3 3.5 %copy.12 = bf16[1,320,4096]{2,1,0:T(8,128)(2,1)} copy(bf16[1,320,4096]{2,1,0:T(8,128)(2,1)} %shard_map.82) | data formatting | bytes 5242880

commit v2 on v1

--- a/solution.py
+++ b/solution.py
@@ -56,6 +56,7 @@
     lwbuf,
     fbuf,
     wbuf,
+    relay,
     thr,
     loc_sem,
     qrecv,
@@ -69,6 +70,8 @@
     hrecv,
     hsend,
     tsend,
+    rsend,
+    rrecv,
 ):
     nz = n // ny
     rows = q_hbm.shape[1]
@@ -114,7 +117,7 @@
         copy.start()
     pltpu.make_async_copy(q_hbm.at[0, :, columns(me)], qbuf.at[0], qrecv.at[0]).start()
 
-    wbuf[0] = jnp.full((8, HD), win_ref[0, 0].astype(jnp.float32))
+    wbuf[me] = jnp.full((8, HD), win_ref[0, 0].astype(jnp.float32))
 
     barrier = pltpu.get_barrier_semaphore()
 
@@ -127,51 +130,63 @@
         pl.semaphore_signal(barrier, 1, device_id={"section": other, "seq": me}, device_id_type=MESH)
     pl.semaphore_wait(barrier, n + 1)
 
+    wide = q_hbm.shape[2]
+    quarter = wide // ny
+    lead = pl.ds(0, LEAD)
+    last = pl.ds(rows - LEAD, LEAD)
+    fresh = (k_hbm, v_hbm)
+    caches = (kc_hbm, vc_hbm)
+    wholes = (kall, vall)
+    edge = y == ny - 1
+    ahead = z < nz - 1
+
+    parts = n // 2
+    piece = wide // parts
+    per = parts // ny
+
+    def send_window(i, carry):
+        remote(wbuf.at[me], wbuf.at[me], wsend, wrecv, peer(i)).start()
+        return carry
+
     def send_queries(i, carry):
         p = peer(i)
-        remote(wbuf.at[0], wbuf.at[i], wsend, wrecv, p).start()
         remote(q_hbm.at[0, :, columns(p)], qbuf.at[i], qsend, qrecv.at[i], p).start()
+        at_part = i - 1
+        part = pl.ds(pl.multiple_of(at_part * piece, HD), piece)
+        column = lax.div(at_part, per)
+        by_relay = edge & (column < ny - 1)
+
+        @pl.when((at_part < parts) & by_relay & ahead)
+        def _():
+            held = pl.ds(pl.multiple_of(lax.rem(at_part, per) * piece, HD), piece)
+            for j in range(2):
+                remote(
+                    fresh[j].at[0, last, part], relay.at[j, :, held], rsend, rrecv, z * ny + column
+                ).start()
+
+        @pl.when((at_part < parts) & jnp.logical_not(by_relay) & (me < n - 1))
+        def _():
+            for j in range(2):
+                remote(
+                    fresh[j].at[0, last, part], wholes[j].at[lead, part], hsend.at[j], hrecv.at[j], me + 1
+                ).start()
+
         return carry
 
-    lax.fori_loop(1, n, send_queries, 0)
-
-    halo = []
-    tail = []
-    own_tail = []
-    for j, (fresh, cache, whole) in enumerate(((k_hbm, kc_hbm, kall), (v_hbm, vc_hbm, vall))):
-        halo.append(
-            remote(
-                fresh.at[0, pl.ds(rows - LEAD, LEAD)],
-                whole.at[pl.ds(0, LEAD)],
-                hsend.at[j],
-                hrecv.at[j],
-                lax.rem(me + 1, n),
-            )
-        )
-        for w in range(WMAX - 1):
-            block = cache.at[0, cached - WMAX + 1 + w]
-            place = pl.ds(w * BLK, BLK)
-            tail.append(
-                remote(block, whole.at[place, columns(me)], tsend.at[j, w], hrecv.at[j], 0)
-            )
-            own_tail.append(
-                pltpu.make_async_copy(block, whole.at[place, pl.ds(0, HD)], hrecv.at[j])
-            )
-
-    @pl.when(me < n - 1)
-    def _():
-        for copy in halo:
-            copy.start()
-
-    @pl.when(me > 0)
-    def _():
-        for copy in tail:
-            copy.start()
+    head_start = min(5, n)
+    lax.fori_loop(1, head_start, send_queries, 0)
+    lax.fori_loop(1, n, send_window, 0)
+    lax.fori_loop(head_start, n, send_queries, 0)
 
     @pl.when(me == 0)
     def _():
-        for copy in own_tail:
-            copy.start()
+        for j in range(2):
+            for w in range(WMAX - 1):
+                pltpu.make_async_copy(
+                    caches[j].at[0, cached - WMAX + 1 + w],
+                    wholes[j].at[pl.ds(w * BLK, BLK), pl.ds(0, HD)],
+                    hrecv.at[j],
+                ).start()
 
     row = lax.broadcasted_iota(jnp.int32, (BLK, WMAX * BLK), 0)
     col = lax.broadcasted_iota(jnp.int32, (BLK, WMAX * BLK), 1)
@@ -179,9 +194,8 @@
     width = jnp.where(col < BLK, 3.0, jnp.where(col < 2 * BLK, 2.0, jnp.where(late, 99.0, 1.0)))
     thr[...] = width
 
-    def window_part(i, blocks):
-        h = source(i)
-        span = wbuf[i, 0:1, 0:1]
+    def window_part(h, blocks):
+        span = wbuf[h, 0:1, 0:1]
         allowed = thr[...] <= span
         for b in blocks:
             q = qv[b * BLK : (b + 1) * BLK, columns(h)]
@@ -197,20 +211,7 @@
                 top * SCALE2 + jnp.log2(total), (BLK, HD)
             )
 
-    def inner_window(i, carry):
-        window_part(i, range(WMAX - 1, nb))
-        return carry
-
-    def edge_window(i, carry):
-        window_part(i, range(WMAX - 1))
-        return carry
-
-    for copy in local[:3]:
-        copy.wait()
-    pltpu.make_async_copy(wbuf.at[pl.ds(1, n - 1)], wbuf.at[pl.ds(1, n - 1)], wrecv).wait()
-    lax.fori_loop(0, n, inner_window, 0)
-
-    for copy in local[3:]:
+    for copy in local:
         copy.wait()
 
     diagonal = lax.broadcasted_iota(jnp.int32, (BLK, HD), 0) == lax.broadcasted_iota(
@@ -220,6 +221,7 @@
 
     def far_part(i, carry):
         src = source(i)
+
         pltpu.make_async_copy(qbuf.at[i], qbuf.at[i], qrecv.at[i]).wait()
         stats = jnp.zeros((STAT, HD), jnp.float32)
         for b in range(nb):
@@ -249,17 +251,48 @@
         @pl.when(i == 0)
         def _():
             pltpu.make_async_copy(obuf.at[i], ogbuf.at[i], orecv.at[i]).start()
-
+            pltpu.make_async_copy(wbuf.at[pl.ds(1, n - 1)], wbuf.at[pl.ds(1, n - 1)], wrecv).wait()
+
+        turn = i - min(4, n // 2)
+
+        @pl.when((turn == 0) & jnp.logical_not(edge) & ahead)
+        def _():
+            pltpu.make_async_copy(relay, relay, rrecv).wait()
+
+        @pl.when((turn >= 0) & (turn < quarter // HD) & jnp.logical_not(edge) & ahead)
+        def _():
+            for j in range(2):
+                remote(
+                    relay.at[j, :, columns(turn)],
+                    wholes[j].at[lead, columns(y * (quarter // HD) + turn)],
+                    rsend,
+                    hrecv.at[j],
+                    (z + 1) * ny,
+                ).start()
+
+        @pl.when((i == 1 + lax.div(me, ny * 2)) & (me > 0))
+        def _():
+            for j in range(2):
+                for w in range(WMAX - 1):
+                    remote(
+                        caches[j].at[0, cached - WMAX + 1 + w],
+                        wholes[j].at[pl.ds(w * BLK, BLK), columns(me)],
+                        tsend,
+                        hrecv.at[j],
+                        0,
+                    ).start()
+
+        window_part(src, range(WMAX - 1, nb))
         return carry
 
     lax.fori_loop(0, n, far_part, 0)
 
     for j, whole in enumerate((kall, vall)):
         pltpu.make_async_copy(whole.at[pl.ds(0, LEAD)], whole.at[pl.ds(0, LEAD)], hrecv.at[j]).wait()
-    lax.fori_loop(0, n, edge_window, 0)
 
     def join(i, carry):
         h = peer(i)
+        window_part(h, range(WMAX - 1))
         pltpu.make_async_copy(ogbuf.at[i], ogbuf.at[i], orecv.at[i]).wait()
         stats = ogbuf[i, nb * BLK : nb * BLK + STAT, :].astype(jnp.float32)
         for b in range(nb):
@@ -281,15 +314,26 @@
     pltpu.make_async_copy(fbuf, fbuf, fsend).wait()
     pltpu.make_async_copy(out_hbm.at[0], out_hbm.at[0], frecv).wait()
 
-    @pl.when(me < n - 1)
+    @pl.when(jnp.logical_not(edge))
     def _():
-        for copy in halo:
-            copy.wait_send()
+        for j, whole in enumerate(wholes):
+            pltpu.make_async_copy(whole.at[lead], whole.at[lead], hsend.at[j]).wait()
+
+    @pl.when(edge & ahead)
+    def _():
+        for j in range(2):
+            pltpu.make_async_copy(relay.at[j], relay.at[j], hsend.at[j]).wait()
+        sent = kall.at[pl.ds(0, 2 * LEAD), pl.ds(0, (ny - 1) * quarter)]
+        pltpu.make_async_copy(sent, sent, rsend).wait()
+
+    @pl.when(jnp.logical_not(edge) & ahead)
+    def _():
+        pltpu.make_async_copy(relay, relay, rsend).wait()
 
     @pl.when(me > 0)
     def _():
-        for copy in tail:
-            copy.wait_send()
+        sent = kcv.at[pl.ds(0, 2 * (WMAX - 1))]
+        pltpu.make_async_copy(sent, sent, tsend).wait()
 
 
 def per_device(n, ny, sections, q, k, v, kc, vc, window, glob, rand):
@@ -317,6 +361,7 @@
             pltpu.VMEM((n, rows, HD), f32),
             pltpu.VMEM((n, rows, HD), bf),
             pltpu.VMEM((n, 8, HD), f32),
+            pltpu.VMEM((2, LEAD, wide // ny), bf),
             pltpu.VMEM((BLK, WMAX * BLK), f32),
             dma((5,)),
             dma((n,)),
@@ -329,7 +374,9 @@
             dma,
             dma((2,)),
             dma((2,)),
-            dma((2, WMAX - 1)),
+            dma,
+            dma,
+            dma,
         ],
         compiler_params=pltpu.CompilerParams(
             collective_id=0, has_side_effects=True, vmem_limit_bytes=56 * 1024 * 1024

time: 200 us -> 161 us (0.81)
  Pallas kernels: 192 us -> 155 us
    pallas_call x1, Pallas kernels: 192 us -> 155 us  [per_device(): pl.pallas_call(functools.partial(kernel, n, ny, sections), out_shape=jax....]
where the time goes in v2:
time: 161 us; the launch traced here: 160 us
  Pallas kernels  155 us (96%)
  local copies, waits for them, and re-layouts  4.96 us (3%)
    pallas_call x1, Pallas kernels, per_device(): pl.pallas_call(functools.partial(kernel, n, ny, sections), out_shape=jax....  155 us
    unnamed x2, local copies, waits for them, and re-layouts  4.96 us

profile of v2, /device:TPU:88, one launch (start us, length us, event | category | flops | bytes accessed | tf_op | source)
XLA Modules:
  0.0 160.3 jit_solution(5742982396680476129)
XLA Ops:
  0.7 1.4 copy.9.rand_ref
  2.1 154.7 %shard_map.82 = bf16[1,320,4096]{2,1,0:T(8,128)(2,1)} custom-call(bf16[1,320,4096]{2,1,0:T(8,128)(2,1)} %q_hbm.1, bf16[1,320,4096]{2,1,0:T(8,128)(2,1)} %k_hbm.1, bf16[1,320,4096]{2,1,0:T(8,128)(2,1)} %v_hbm.1, bf16[1,96,64,128]{3,2,1,0:T(8,128)(2,1)} %bitcast.2, bf16[1,96,64,128]{3,2,1,0:T(8,128)(2,1)} %bitcast.3, s32[1,1]{1,0:T(1,128)S(6)} %copy.11.win_ref, ...), custom_call_target="tpu_custom_call" | custom-call | tf_op jit(solution)/shard_map/pallas_call | solution.py:346
  156.8 3.5 %copy.12 = bf16[1,320,4096]{2,1,0:T(8,128)(2,1)} copy(bf16[1,320,4096]{2,1,0:T(8,128)(2,1)} %shard_map.82) | data formatting | bytes 5242880

commit v3 on v2

--- a/solution.py
+++ b/solution.py
@@ -69,7 +69,6 @@
     wrecv,
     hrecv,
     hsend,
-    tsend,
     rsend,
     rrecv,
 ):
@@ -135,7 +134,6 @@
     lead = pl.ds(0, LEAD)
     last = pl.ds(rows - LEAD, LEAD)
     fresh = (k_hbm, v_hbm)
-    caches = (kc_hbm, vc_hbm)
     wholes = (kall, vall)
     edge = y == ny - 1
     ahead = z < nz - 1
@@ -144,9 +142,20 @@
     piece = wide // parts
     per = parts // ny
 
-    def send_window(i, carry):
-        remote(wbuf.at[me], wbuf.at[me], wsend, wrecv, peer(i)).start()
-        return carry
+    plane = wbuf.at[pl.ds(pl.multiple_of(z * ny, ny), ny)]
+
+    def send_window_y(i, carry):
+        near = z * ny + lax.rem(y + i, ny)
+        remote(wbuf.at[me], wbuf.at[me], wsend.at[0], wrecv.at[0], near).start()
+        return carry
+
+    def send_window_z(i, carry):
+        far = lax.rem(z + i, nz) * ny + y
+        remote(plane, plane, wsend.at[1], wrecv.at[1], far).start()
+        return carry
+
+    def tiles(count, sem):
+        pltpu.make_async_copy(wbuf.at[pl.ds(0, count)], wbuf.at[pl.ds(0, count)], sem).wait()
 
     def send_queries(i, carry):
         p = peer(i)
@@ -173,31 +182,30 @@
 
         return carry
 
-    head_start = min(5, n)
+    head_start = min(9, n)
+    lax.fori_loop(1, ny, send_window_y, 0)
     lax.fori_loop(1, head_start, send_queries, 0)
-    lax.fori_loop(1, n, send_window, 0)
+    tiles(ny - 1, wrecv.at[0])
+    lax.fori_loop(1, nz, send_window_z, 0)
     lax.fori_loop(head_start, n, send_queries, 0)
 
     @pl.when(me == 0)
     def _():
-        for j in range(2):
-            for w in range(WMAX - 1):
-                pltpu.make_async_copy(
-                    caches[j].at[0, cached - WMAX + 1 + w],
-                    wholes[j].at[pl.ds(w * BLK, BLK), pl.ds(0, HD)],
-                    hrecv.at[j],
-                ).start()
+        for whole in wholes:
+            whole[lead, :] = jnp.zeros((LEAD, wide), jnp.bfloat16)
 
     row = lax.broadcasted_iota(jnp.int32, (BLK, WMAX * BLK), 0)
     col = lax.broadcasted_iota(jnp.int32, (BLK, WMAX * BLK), 1)
     late = col - (WMAX - 1) * BLK > row
     width = jnp.where(col < BLK, 3.0, jnp.where(col < 2 * BLK, 2.0, jnp.where(late, 99.0, 1.0)))
-    thr[...] = width
+    for b in range(WMAX):
+        unseen = jnp.where(me == 0, (WMAX - 1 - b) * BLK, 0)
+        thr[b] = jnp.where(col < unseen, 99.0, width)
 
     def window_part(h, blocks):
         span = wbuf[h, 0:1, 0:1]
-        allowed = thr[...] <= span
         for b in blocks:
+            allowed = thr[min(b, WMAX - 1)] <= span
             q = qv[b * BLK : (b + 1) * BLK, columns(h)]
             k = kall[b * BLK : b * BLK + WMAX * BLK, columns(h)]
             v = vall[b * BLK : b * BLK + WMAX * BLK, columns(h)]
@@ -219,18 +227,23 @@
     )
     stat_row = lax.broadcasted_iota(jnp.int32, (STAT, HD), 0)
 
-    def far_part(i, carry):
-        src = source(i)
-
-        pltpu.make_async_copy(qbuf.at[i], qbuf.at[i], qrecv.at[i]).wait()
+    span_here = win_ref[0, 0].astype(jnp.float32)
+
+    def far_chunk(i, src, opening):
         stats = jnp.zeros((STAT, HD), jnp.float32)
         for b in range(nb):
             picks = [glob_ref[0, g] for g in range(GLOB)] + [
-                rand_ref[0, src * nb + b, r] for r in range(RAND)
+                rand_ref[r, 0, src * nb + b] for r in range(RAND)
             ]
+            extra = WMAX - 1 - b if opening and b < WMAX - 1 else 0
+            picks += [cached - extra + w for w in range(extra)]
             k = jnp.concatenate([kcv[x] for x in picks], axis=0)
             v = jnp.concatenate([vcv[x] for x in picks], axis=0)
             s = nt_dot(qbuf[i, b * BLK : (b + 1) * BLK, :], k)
+            if extra:
+                place = lax.broadcasted_iota(jnp.int32, s.shape, 1) - (GLOB + RAND) * BLK
+                least = jnp.where(place < 0, 0.0, jnp.where(place < BLK, 3.0, 2.0))
+                s = jnp.where(least <= span_here, s, MASKED)
             top = jnp.max(s, axis=1, keepdims=True)
             e = jnp.exp2((s - top) * SCALE2)
             total = jnp.sum(e, axis=1, keepdims=True)
@@ -244,6 +257,18 @@
                 line = line - piece
         obuf[i, nb * BLK : nb * BLK + STAT, :] = stats.astype(jnp.bfloat16)
 
+    def far_part(i, carry):
+        src = source(i)
+
+        pltpu.make_async_copy(qbuf.at[i], qbuf.at[i], qrecv.at[i]).wait()
+        @pl.when(src == 0)
+        def _():
+            far_chunk(i, src, True)
+
+        @pl.when(src > 0)
+        def _():
+            far_chunk(i, src, False)
+
         @pl.when(i > 0)
         def _():
             remote(obuf.at[i], ogbuf.at[i], osend, orecv.at[i], src).start()
@@ -251,7 +276,7 @@
         @pl.when(i == 0)
         def _():
             pltpu.make_async_copy(obuf.at[i], ogbuf.at[i], orecv.at[i]).start()
-            pltpu.make_async_copy(wbuf.at[pl.ds(1, n - 1)], wbuf.at[pl.ds(1, n - 1)], wrecv).wait()
+            tiles(n - ny, wrecv.at[1])
 
         turn = i - min(4, n // 2)
 
@@ -270,25 +295,16 @@
                     (z + 1) * ny,
                 ).start()
 
-        @pl.when((i == 1 + lax.div(me, ny * 2)) & (me > 0))
-        def _():
-            for j in range(2):
-                for w in range(WMAX - 1):
-                    remote(
-                        caches[j].at[0, cached - WMAX + 1 + w],
-                        wholes[j].at[pl.ds(w * BLK, BLK), columns(me)],
-                        tsend,
-                        hrecv.at[j],
-                        0,
-                    ).start()
-
         window_part(src, range(WMAX - 1, nb))
         return carry
 
     lax.fori_loop(0, n, far_part, 0)
 
-    for j, whole in enumerate((kall, vall)):
-        pltpu.make_async_copy(whole.at[pl.ds(0, LEAD)], whole.at[pl.ds(0, LEAD)], hrecv.at[j]).wait()
+    @pl.when(me > 0)
+    def _():
+        for j, whole in enumerate(wholes):
+            pltpu.make_async_copy(whole.at[lead], whole.at[lead], hrecv.at[j]).wait()
+
 
     def join(i, carry):
         h = peer(i)
@@ -308,7 +324,8 @@
 
     lax.fori_loop(0, n, join, 0)
 
-    pltpu.make_async_copy(wbuf.at[pl.ds(1, n - 1)], wbuf.at[pl.ds(1, n - 1)], wsend).wait()
+    tiles(ny - 1, wsend.at[0])
+    tiles(n - ny, wsend.at[1])
     pltpu.make_async_copy(qbuf.at[pl.ds(1, n - 1)], qbuf.at[pl.ds(1, n - 1)], qsend).wait()
     pltpu.make_async_copy(obuf.at[pl.ds(1, n - 1)], obuf.at[pl.ds(1, n - 1)], osend).wait()
     pltpu.make_async_copy(fbuf, fbuf, fsend).wait()
@@ -329,11 +346,6 @@
     @pl.when(jnp.logical_not(edge) & ahead)
     def _():
         pltpu.make_async_copy(relay, relay, rsend).wait()
-
-    @pl.when(me > 0)
-    def _():
-        sent = kcv.at[pl.ds(0, 2 * (WMAX - 1))]
-        pltpu.make_async_copy(sent, sent, tsend).wait()
 
 
 def per_device(n, ny, sections, q, k, v, kc, vc, window, glob, rand):
@@ -362,7 +374,7 @@
             pltpu.VMEM((n, rows, HD), bf),
             pltpu.VMEM((n, 8, HD), f32),
             pltpu.VMEM((2, LEAD, wide // ny), bf),
-            pltpu.VMEM((BLK, WMAX * BLK), f32),
+            pltpu.VMEM((WMAX, BLK, WMAX * BLK), f32),
             dma((5,)),
             dma((n,)),
             dma((n,)),
@@ -370,18 +382,17 @@
             dma,
             dma,
             dma,
-            dma,
-            dma,
             dma((2,)),
             dma((2,)),
-            dma,
+            dma((2,)),
+            dma((2,)),
             dma,
             dma,
         ],
         compiler_params=pltpu.CompilerParams(
             collective_id=0, has_side_effects=True, vmem_limit_bytes=56 * 1024 * 1024
         ),
-    )(q, k, v, kc, vc, window, glob, rand)
+    )(q, k, v, kc, vc, window, glob, jnp.transpose(rand, (2, 0, 1)))
 
 
 def solution(mesh):

time: 161 us -> 152 us (0.944)
  Pallas kernels: 155 us -> 148 us
    pallas_call x1, Pallas kernels: 155 us -> 148 us  [per_device(): pl.pallas_call(functools.partial(kernel, n, ny, sections), out_shape=jax....]
    unnamed x2 -> x1, local copies, waits for them, and re-layouts: 4.96 us -> 3.53 us
where the time goes in v3:
time: 152 us
  Pallas kernels  148 us (97%)
  local copies, waits for them, and re-layouts  3.53 us (2%)
    pallas_call x1, Pallas kernels, per_device(): pl.pallas_call(functools.partial(kernel, n, ny, sections), out_shape=jax....  148 us
    unnamed x1, local copies, waits for them, and re-layouts  3.53 us

profile of v3, /device:TPU:88, one launch (start us, length us, event | category | flops | bytes accessed | tf_op | source)
XLA Modules:
  0.0 152.3 jit_solution(4317776060919029856)
XLA Ops:
  0.7 148.1 %shard_map.82 = bf16[1,320,4096]{2,1,0:T(8,128)(2,1)} custom-call(bf16[1,320,4096]{2,1,0:T(8,128)(2,1)} %q_hbm.1, bf16[1,320,4096]{2,1,0:T(8,128)(2,1)} %k_hbm.1, bf16[1,320,4096]{2,1,0:T(8,128)(2,1)} %v_hbm.1, bf16[1,96,64,128]{3,2,1,0:T(8,128)(2,1)} %bitcast.3, bf16[1,96,64,128]{3,2,1,0:T(8,128)(2,1)} %bitcast.4, s32[1,1]{1,0:T(1,128)S(6)} %copy.10.win_ref, ...), custom_call_target="tpu_custom_call" | custom-call | tf_op jit(solution)/shard_map/pallas_call | solution.py:358
  148.8 3.5 %copy.11 = bf16[1,320,4096]{2,1,0:T(8,128)(2,1)} copy(bf16[1,320,4096]{2,1,0:T(8,128)(2,1)} %shard_map.82) | data formatting | bytes 5242880

commit v4 on v3

--- a/solution.py
+++ b/solution.py
@@ -278,7 +278,7 @@
             pltpu.make_async_copy(obuf.at[i], ogbuf.at[i], orecv.at[i]).start()
             tiles(n - ny, wrecv.at[1])
 
-        turn = i - min(4, n // 2)
+        turn = i - min(2, n // 2)
 
         @pl.when((turn == 0) & jnp.logical_not(edge) & ahead)
         def _():

time: 152 us -> 150 us (0.987)
  Pallas kernels: 148 us -> 146 us
    pallas_call x1, Pallas kernels: 148 us -> 146 us  [per_device(): pl.pallas_call(functools.partial(kernel, n, ny, sections), out_shape=jax....]
where the time goes in v4:
time: 150 us
  Pallas kernels  146 us (97%)
  local copies, waits for them, and re-layouts  3.53 us (2%)
    pallas_call x1, Pallas kernels, per_device(): pl.pallas_call(functools.partial(kernel, n, ny, sections), out_shape=jax....  146 us
    unnamed x1, local copies, waits for them, and re-layouts  3.53 us

profile of v4, /device:TPU:88, one launch (start us, length us, event | category | flops | bytes accessed | tf_op | source)
XLA Modules:
  0.0 150.0 jit_solution(2535119932975445015)
XLA Ops:
  0.7 145.8 %shard_map.82 = bf16[1,320,4096]{2,1,0:T(8,128)(2,1)} custom-call(bf16[1,320,4096]{2,1,0:T(8,128)(2,1)} %q_hbm.1, bf16[1,320,4096]{2,1,0:T(8,128)(2,1)} %k_hbm.1, bf16[1,320,4096]{2,1,0:T(8,128)(2,1)} %v_hbm.1, bf16[1,96,64,128]{3,2,1,0:T(8,128)(2,1)} %bitcast.3, bf16[1,96,64,128]{3,2,1,0:T(8,128)(2,1)} %bitcast.4, s32[1,1]{1,0:T(1,128)S(6)} %copy.10.win_ref, ...), custom_call_target="tpu_custom_call" | custom-call | tf_op jit(solution)/shard_map/pallas_call | solution.py:358
  146.5 3.5 %copy.11 = bf16[1,320,4096]{2,1,0:T(8,128)(2,1)} copy(bf16[1,320,4096]{2,1,0:T(8,128)(2,1)} %shard_map.82) | data formatting | bytes 5242880
